TPU v7x, 32 devices: a whole 2x2x4 slice. The times are simulated.
32 devices in a mesh: row: 4 (over y, x), col: 8 (over z, core).
Axes of the slice: x: 2, y: 2, z: 4, core: 2. Of those that a mesh axis runs over, the one named last changes fastest.
Arguments:
- factor: bfloat16 [4096, 131072], P('row', 'col'), may hold values from -0.015625 to 0.015625
- panels: bfloat16 [131072, 256], P('col', 'row'), may hold values from -6 to 6
- base_demand: float32 [4096], replicated, may hold values from 0.3 to 3
- spread: float32 [4096], replicated, may hold values from 0.1 to 0.6
- head_base: float32 [4096], replicated, may hold values from -8 to 8
- head_drop: float32 [4096], replicated, may hold values from 0.2 to 1
- conductance: float32 [8192], replicated, may hold values from 0.3 to 1.5
- pipe_ends: int32 [8192, 2], replicated, may hold values from 0 to 4095
Outputs:
- imbalance: float32 [256, 4096], P(('col', 'row'))
All inputs are finite; a program needn't handle non-finite values.
Results may differ from a plain program's by a relative error of at most 0.0003.
Values may be sent and summed in bfloat16 or wider, within the bound.
A program may use at most 128 MiB of HBM per device.

v0:
```python
import jax
import jax.numpy as jnp
from jax import lax
from jax.sharding import PartitionSpec as P

NODES = 131072


def regroup_rows(shares):
    return lax.all_to_all(shares, "row", split_axis=0, concat_axis=1, tiled=True)


def shards(factor, panels, base_demand, spread, head_base, head_drop, conductance, pipe_ends):
    local_rows = factor.shape[0]
    width = factor.shape[1]
    n_row = lax.axis_size("row")
    n_col = lax.axis_size("col")
    slab = local_rows * n_row
    offset = NODES - slab
    rows = (
        lax.broadcasted_iota(jnp.int32, factor.shape, 0)
        + offset
        + lax.axis_index("row") * local_rows
    )
    cols = lax.broadcasted_iota(jnp.int32, factor.shape, 1) + lax.axis_index("col") * width
    kept = jnp.where(cols <= rows, factor, jnp.zeros_like(factor))
    partial_scores = lax.dot_general(
        lax.all_gather(panels, "row", axis=1, tiled=True),
        kept,
        (((0,), (1,)), ((), ())),
        preferred_element_type=jnp.float32,
    )
    total = partial_scores.shape[0]
    share = total // n_col
    summed = lax.psum(partial_scores, "col")
    mine = lax.dynamic_slice_in_dim(summed, lax.axis_index("col") * share, share, 0)
    scores = regroup_rows(mine)
    demand = base_demand * jnp.exp(spread * scores)
    heads = head_base - head_drop * demand
    starts = pipe_ends[:, 0]
    ends = pipe_ends[:, 1]
    diff = jnp.take(heads, starts, axis=1) - jnp.take(heads, ends, axis=1)
    flow = conductance * jnp.sign(diff) * jnp.abs(diff) ** 0.54
    inflow = jnp.zeros_like(demand).at[:, ends].add(flow).at[:, starts].add(-flow)
    return inflow - demand


def solution(mesh):
    return jax.shard_map(
        shards,
        mesh=mesh,
        in_specs=(P("row", "col"), P("col", "row"), P(), P(), P(), P(), P(), P()),
        out_specs=P(("col", "row"), None),
        check_vma=False,
    )
```

profile of v0, /device:TPU:0, one launch (start us, length us, event | category | flops | bytes accessed | tf_op | source)
XLA Modules:
  0.0 353.8 jit_solution(14936233553656885815)
XLA Ops:
  6.5 0.0 all-gather.2.cloned.1.call-start
  6.5 0.7 all-gather.2.cloned.1.call-update
  7.3 0.0 all-reduce.2.cloned.1.call-start
  7.3 0.0 copy-start
  7.4 0.0 copy-start.1
  7.4 0.0 copy-start.2
  7.4 0.0 copy-start.4
  7.4 0.0 copy-start.5
  7.4 92.1 %all-gather.2.cloned.1.call-done = bf16[16384,256]{0,1:T(8,128)(2,1)} async-done(((bf16[16384,64]{0,1:T(8,128)(2,1)}), bf16[16384,256]{0,1:T(8,128)(2,1)}) %all-gather.2.cloned.1.call-update) | async-done | bytes 8388624 | tf_op jit(solution)/shard_map/all_gather | solution.py:28
  99.5 19.0 %fusion.4 = f32[256,1024]{0,1:T(8,128)} fusion(bf16[16384,256]{0,1:T(8,128)(2,1)} %all-gather.2.cloned.1.call-done, bf16[1024,16384]{1,0:T(8,128)(2,1)} %param.10, s32[16384]{0:T(1024)S(1)} %iota_add_fusion, s32[1024]{0:T(1024)S(1)} %add_add_fusion), kind=kOutput, calls=%fused_computation.9 | convolution fusion | flops 8623489024 | bytes 43061248 | tf_op jit(solution)/shard_map/dot_general | solution.py:27
  118.6 0.0 all-reduce.2.cloned.1.call-update
  118.6 0.0 copy-done
  118.6 0.1 compare_select_fusion.4
  118.8 58.8 %all-reduce.2.cloned.1.call-done = f32[256,1024]{0,1:T(8,128)} async-done(((f32[256,1024]{0,1:T(8,128)}), f32[256,1024]{0,1:T(8,128)}) %all-reduce.2.cloned.1.call-update) | async-done | bytes 1048592 | tf_op jit(solution)/shard_map/psum | solution.py:35
  177.5 1.2 constant_dynamic-slice_fusion
  178.8 0.8 copy.13
  179.6 3.6 %all-to-all-start = ((f32[4,8,1024]{2,1,0:T(8,128)}), f32[4,8,1024]{2,1,0:T(8,128)S(1)}, u32[]{:S(2)}, u32[]{:S(2)}) async-start(f32[4,8,1024]{2,1,0:T(8,128)} %bitcast.3), calls=%async_computation | async-start | bytes 262144 | tf_op jit(solution)/shard_map/all_to_all | solution.py:10
  183.2 5.0 %all-to-all-done = f32[4,8,1024]{2,1,0:T(8,128)S(1)} async-done(((f32[4,8,1024]{2,1,0:T(8,128)}), f32[4,8,1024]{2,1,0:T(8,128)S(1)}, u32[]{:S(2)}, u32[]{:S(2)}) %all-to-all-start) | async-done | bytes 131104 | tf_op jit(solution)/shard_map/all_to_all | solution.py:10
  188.2 0.0 copy-done.1
  188.2 0.0 copy-done.2
  188.3 0.0 copy-done.4
  188.3 0.0 copy-done.5
  188.3 0.6 copy.14
  188.9 27.9 %gather_fusion = f32[8192,8]{1,0:T(8,128)} fusion(f32[8,4096]{0,1:T(8,128)S(1)} %copy.14, s32[8192]{0:T(1024)S(1)} %fusion.8), kind=kCustom, calls=%fused_computation.clone | custom fusion | bytes 557056 | tf_op jit(solution)/shard_map/jit(_take)/gather | solution.py:42
  216.8 2.8 copy.15
  219.6 0.0 copy-start.3
  219.6 27.9 %gather_fusion.1 = f32[8192,8]{1,0:T(8,128)} fusion(f32[8,4096]{0,1:T(8,128)S(1)} %copy.14, s32[8192]{0:T(1024)S(1)} %fusion.9), kind=kCustom, calls=%fused_computation.1.clone | custom fusion | bytes 557056 | tf_op jit(solution)/shard_map/jit(_take)/gather | solution.py:42
  247.5 2.8 copy.17
  250.3 0.0 copy-done.3
  250.3 0.3 negate_bitcast_fusion
  250.6 2.6 copy.18
  253.2 2.6 copy.19
  255.8 44.8 %scatter_custom_fusion = f32[8,4096]{0,1:T(8,128)S(1)} fusion(s32[8192]{0:T(1024)S(1)} %bitcast.38, f32[8192,8]{1,0:T(8,128)} %copy.18, f32[]{:T(128)} %constant.3.clone.1), kind=kCustom, calls=%fused_computation.10 | custom fusion | flops 65536 | bytes 131584 | tf_op jit(solution)/shard_map/scatter-add | solution.py:44
  300.6 45.1 %scatter_fusion = f32[8,4096]{0,1:T(8,128)S(1)} fusion(f32[8,4096]{0,1:T(8,128)S(1)} %scatter_custom_fusion, s32[8192]{0:T(1024)S(1)} %bitcast.37, f32[8192,8]{1,0:T(8,128)} %copy.19), kind=kCustom, calls=%fused_computation.3 | custom fusion | flops 65536 | bytes 819200 | tf_op jit(solution)/shard_map/scatter-add | solution.py:44
  345.7 0.6 copy.20
  346.3 0.7 fusion.7
  (6 shorter events, 0.1 us)
Async XLA Ops:
  6.5 93.0 %all-gather.2.cloned.1.call-start = ((), (), s32[]{:S(2)}) async-start(), calls=%async_computation.1 | async-start | bytes 10485760 | tf_op jit(solution)/shard_map/all_gather | solution.py:28
  7.3 170.3 %all-reduce.2.cloned.1.call-start = ((), (), s32[]{:S(2)}) async-start(), calls=%async_computation.2 | async-start | bytes 2097152 | tf_op jit(solution)/shard_map/psum | solution.py:35
  7.3 111.3 %copy-start = (s32[8192,2]{0,1:T(2,128)S(1)}, s32[8192,2]{0,1:T(2,128)}, u32[]{:S(2)}) copy-start(s32[8192,2]{0,1:T(2,128)} %param.17) | copy-start | bytes 196612
  7.4 180.9 %copy-start.1 = (f32[4096]{0:T(1024)S(1)}, f32[4096]{0:T(1024)}, u32[]{:S(2)}) copy-start(f32[4096]{0:T(1024)} %param.13) | copy-start | bytes 49156
  7.4 180.9 %copy-start.2 = (f32[4096]{0:T(1024)S(1)}, f32[4096]{0:T(1024)}, u32[]{:S(2)}) copy-start(f32[4096]{0:T(1024)} %param.12) | copy-start | bytes 49156
  7.4 180.9 %copy-start.4 = (f32[4096]{0:T(1024)S(1)}, f32[4096]{0:T(1024)}, u32[]{:S(2)}) copy-start(f32[4096]{0:T(1024)} %param.15) | copy-start | bytes 49156
  7.4 180.9 %copy-start.5 = (f32[4096]{0:T(1024)S(1)}, f32[4096]{0:T(1024)}, u32[]{:S(2)}) copy-start(f32[4096]{0:T(1024)} %param.14) | copy-start | bytes 49156
  179.6 8.6 %all-to-all-start = ((f32[4,8,1024]{2,1,0:T(8,128)}), f32[4,8,1024]{2,1,0:T(8,128)S(1)}, u32[]{:S(2)}, u32[]{:S(2)}) async-start(f32[4,8,1024]{2,1,0:T(8,128)} %bitcast.3), calls=%async_computation | async-start | bytes 262144 | tf_op jit(solution)/shard_map/all_to_all | solution.py:10
  219.6 30.7 %copy-start.3 = (f32[8192]{0:T(1024)S(1)}, f32[8192]{0:T(1024)}, u32[]{:S(2)}) copy-start(f32[8192]{0:T(1024)} %param.16) | copy-start | bytes 98308
Sparse Core Ops, SparseCore 0:
  9.2 90.2 all-gather.1
  118.7 58.7 all-reduce.1
where the time goes:
time: 354 us
  waiting for transfers between devices  157 us (44%)
  other arithmetic  91.1 us (26%)
  local copies, waits for them, and re-layouts  69.9 us (20%)
  matrix products  19 us (5%)
  between operations  13.6 us (4%)
  starting transfers between devices  3.66 us (1%)
    all_gather x1, waiting for transfers between devices, shards(): lax.all_gather(panels, 'row', axis=1, tiled=True)  92.1 us
    scatter-add x2, other arithmetic, shards(): jnp.zeros_like(demand).at[:, ends].add(flow).at[:, starts].add(-flow)  89.9 us
    gather x4, local copies, waits for them, and re-layouts, shards(): diff = jnp.take(heads, starts, axis=1) - jnp.take(heads, ends, axis=1)  61.4 us
    psum x1, waiting for transfers between devices, shards(): summed = lax.psum(partial_scores, 'col')  58.8 us
    dot_general x1, matrix products, shards(): lax.dot_general(lax.all_gather(panels, 'row', axis=1, tiled=True), kept,...  19 us
  transfers between devices with their start and end apart: 3, of which 3 were waited for; matrix products, arithmetic and copies ran while one was open for 0% of the time, Pallas kernels for 0%

commit v1 on v0

v1 whole, which is shorter than its diff:
```python
import functools

import jax
import jax.numpy as jnp
from jax import lax
from jax.experimental import pallas as pl
from jax.experimental.pallas import tpu as pltpu
from jax.sharding import PartitionSpec as P

NODES = 131072
LO = 256
PIPE_BLOCK = 1024
HALVES = 2


def split_bf16(x, parts):
    pieces = []
    for _ in range(parts):
        piece = x.astype(jnp.bfloat16).astype(jnp.float32)
        pieces.append(piece)
        x = x - piece
    return pieces


def residual_kernel(scores_ref, base_ref, spread_ref, head_ref, drop_ref, cond_ref, ends_ref, out_ref, heads_sc, demand_sc, acc_sc, hot_sc, lhs_sc):
    blocks, count, local = scores_ref.shape
    slab = blocks * local
    groups = slab // LO
    step = pl.program_id(0)
    rows = groups * count

    @pl.when(step == 0)
    def _():
        acc_sc[...] = jnp.zeros_like(acc_sc)
        for b in range(blocks):
            at = pl.ds(b * local, local)
            demand = base_ref[:, at] * jnp.exp(spread_ref[:, at] * scores_ref[b])
            demand_sc[:, at] = demand
            heads = head_ref[:, at] - drop_ref[:, at] * demand
            pieces = split_bf16(heads, 3)
            for p, piece in enumerate(pieces):
                for g in range(local // LO):
                    row = p * rows + (b * (local // LO) + g) * count
                    heads_sc[row : row + count, :] = piece[:, g * LO : (g + 1) * LO]

    width = ends_ref.shape[1]
    table = heads_sc[...].astype(jnp.bfloat16)
    lo_iota = lax.broadcasted_iota(jnp.int32, (LO, width), 0)
    picked = []
    groups_of = []
    for end in range(2):
        node = ends_ref[end : end + 1, :]
        lo = node & (LO - 1)
        hi = jnp.broadcast_to(node >> 8, (count, width))
        hot_sc[end] = jnp.where(lo_iota == lo, 1.0, 0.0).astype(jnp.bfloat16)
        found = jnp.dot(table, hot_sc[end], preferred_element_type=jnp.float32)
        found = found[:rows] + found[rows : 2 * rows] + found[2 * rows :]
        value = jnp.zeros((count, width), jnp.float32)
        for g in range(groups):
            value = jnp.where(hi == g, found[g * count : (g + 1) * count], value)
        picked.append(value)
        groups_of.append(hi)
    diff = picked[0] - picked[1]
    size = jnp.abs(diff)
    live = size > 0.0
    power = jnp.exp(0.54 * jnp.log(jnp.where(live, size, 1.0)))
    flow = cond_ref[...] * jnp.where(live, jnp.where(diff > 0.0, power, -power), 0.0)
    for end in range(2):
        pieces = split_bf16(-flow if end == 0 else flow, 2)
        spread_out = [
            jnp.where(groups_of[end] == g, piece, 0.0)
            for piece in pieces
            for g in range(groups)
        ]
        lhs_sc[end] = jnp.concatenate(spread_out, axis=0).astype(jnp.bfloat16)
        acc_sc[...] += lax.dot_general(hot_sc[end], lhs_sc[end], (((1,), (1,)), ((), ())), preferred_element_type=jnp.float32)

    @pl.when(step == pl.num_programs(0) - 1)
    def _():
        for g in range(groups):
            at = slice(g * LO, (g + 1) * LO)
            if g == 0:
                turned = acc_sc[...].T
            total = turned[g * count : (g + 1) * count, :] + turned[rows + g * count : rows + (g + 1) * count, :]
            out_ref[:, at] = total - demand_sc[:, at]


def residual(scores, base_demand, spread, head_base, head_drop, conductance, pipe_ends):
    blocks, count, local = scores.shape
    slab = blocks * local
    pipes = conductance.shape[0]
    rows = slab // LO * count
    whole = lambda shape: pl.BlockSpec(shape, lambda e: (0,) * len(shape))
    return pl.pallas_call(
        residual_kernel,
        grid=(pipes // PIPE_BLOCK,),
        out_shape=jax.ShapeDtypeStruct((count, slab), jnp.float32),
        in_specs=[
            whole((blocks, count, local)),
            whole((1, slab)),
            whole((1, slab)),
            whole((1, slab)),
            whole((1, slab)),
            pl.BlockSpec((1, PIPE_BLOCK), lambda e: (0, e)),
            pl.BlockSpec((2, PIPE_BLOCK), lambda e: (0, e)),
        ],
        out_specs=whole((count, slab)),
        scratch_shapes=[
            pltpu.VMEM((3 * rows, LO), jnp.float32),
            pltpu.VMEM((count, slab), jnp.float32),
            pltpu.VMEM((LO, 2 * rows), jnp.float32),
            pltpu.VMEM((2, LO, PIPE_BLOCK), jnp.bfloat16),
            pltpu.VMEM((2, 2 * rows, PIPE_BLOCK), jnp.bfloat16),
        ],
        compiler_params=pltpu.CompilerParams(dimension_semantics=("arbitrary",), vmem_limit_bytes=48 * 1024 * 1024),
    )(
        scores,
        base_demand[None, :],
        spread[None, :],
        head_base[None, :],
        head_drop[None, :],
        conductance[None, :],
        pipe_ends.T,
    )


CHUNKS = 4
MESH = pl.DeviceIdType.MESH


def gather_kernel(panels_ref, factor_ref, out_ref, draws, kept, own_sem, factor_sem, send_sem, recv_sem):
    drawn, width = panels_ref.shape
    local_rows = factor_ref.shape[0]
    half = drawn // 2
    span = width // CHUNKS
    me = lax.axis_index("row")
    beside = me + 1 - 2 * (me % 2)
    across = me + 2 - 4 * (me // 2)
    order = (me, beside, across, 3 - me)

    barrier = pltpu.get_barrier_semaphore()
    for peer in (beside, across):
        pl.semaphore_signal(barrier, inc=1, device_id={"row": peer}, device_id_type=MESH)
    pl.semaphore_wait(barrier, 2)

    def at(block, part, c):
        return draws.at[pl.ds(block * drawn + part * half, half), pl.ds(c * span, span)]

    def send(kind, c, source, target, peer):
        return pltpu.make_async_remote_copy(
            src_ref=source,
            dst_ref=target,
            send_sem=send_sem.at[kind, c],
            recv_sem=recv_sem.at[kind, c],
            device_id={"row": peer},
            device_id_type=MESH,
        )

    def mine(part, c):
        return panels_ref.at[pl.ds(part * half, half), pl.ds(c * span, span)]

    sends = []
    for c in range(CHUNKS):
        sends.append(
            (
                send(0, c, mine(0, c), at(1, 0, c), beside),
                send(1, c, mine(1, c), at(2, 1, c), across),
                send(2, c, mine(1, c), at(1, 1, c), beside),
                send(3, c, mine(0, c), at(2, 0, c), across),
                send(4, c, at(1, 0, c), at(3, 0, c), across),
                send(5, c, at(2, 1, c), at(3, 1, c), beside),
            )
        )

    def start(c):
        for copy in sends[c][:4]:
            copy.start()

    def forward(c):
        sends[c][0].wait_recv()
        sends[c][4].start()
        sends[c][1].wait_recv()
        sends[c][5].start()

    start(0)
    start(1)
    own = pltpu.make_async_copy(panels_ref, draws.at[pl.ds(0, drawn), :], own_sem)
    own.start()
    loads = []
    for c in range(CHUNKS):
        piece = pl.ds(c * span, span)
        loads.append(pltpu.make_async_copy(factor_ref.at[:, piece], kept.at[:, piece], factor_sem.at[c]))
        loads[c].start()
    own.wait()

    first_row = NODES - lax.axis_size("row") * local_rows + me * local_rows
    strip = 64
    tile = 256
    forward(0)
    for c in range(CHUNKS):
        if c + 2 < CHUNKS:
            start(c + 2)
        first_col = lax.axis_index("col") * width + c * span
        loads[c].wait()

        @pl.when(first_col + span > first_row)
        def _():
            def mask(t, carry):
                where = pl.ds(pl.multiple_of(t * strip, strip), strip)
                block = kept[where, c * span : (c + 1) * span].astype(jnp.float32)
                row = lax.broadcasted_iota(jnp.int32, block.shape, 0) + (first_row + t * strip)
                col = lax.broadcasted_iota(jnp.int32, block.shape, 1) + first_col
                block = jnp.where(col <= row, block, 0.0)
                kept[where, c * span : (c + 1) * span] = block.astype(jnp.bfloat16)
                return carry

            lax.fori_loop(0, local_rows // strip, mask, 0)

        if c + 1 < CHUNKS:
            forward(c + 1)
        for kind in range(2, 6):
            sends[c][kind].wait_recv()

        def multiply(t, carry):
            where = pl.ds(pl.multiple_of(t * tile, tile), tile)
            found = lax.dot_general(
                draws[:, c * span : (c + 1) * span],
                kept[where, c * span : (c + 1) * span],
                (((1,), (1,)), ((), ())),
                preferred_element_type=jnp.float32,
            )
            for block in range(4):
                rows = pl.ds(pl.multiple_of(order[block] * drawn, drawn), drawn)
                piece = found[block * drawn : (block + 1) * drawn]
                if c == 0:
                    out_ref[rows, where] = piece
                else:
                    out_ref[rows, where] += piece
            return carry

        lax.fori_loop(0, local_rows // tile, multiply, 0)
    for c in range(CHUNKS):
        for copy in sends[c]:
            copy.wait_send()


def gathered_scores(draws, factor):
    drawn, width = draws.shape
    local_rows = factor.shape[0]
    return pl.pallas_call(
        gather_kernel,
        out_shape=jax.ShapeDtypeStruct((4 * drawn, local_rows), jnp.float32),
        in_specs=[pl.BlockSpec(memory_space=pl.ANY)] * 2,
        out_specs=pl.BlockSpec(memory_space=pltpu.VMEM),
        scratch_shapes=[
            pltpu.VMEM((4 * drawn, width), jnp.bfloat16),
            pltpu.VMEM((local_rows, width), jnp.bfloat16),
            pltpu.SemaphoreType.DMA,
            pltpu.SemaphoreType.DMA((CHUNKS,)),
            pltpu.SemaphoreType.DMA((6, CHUNKS)),
            pltpu.SemaphoreType.DMA((6, CHUNKS)),
        ],
        compiler_params=pltpu.CompilerParams(collective_id=0, has_side_effects=True, vmem_limit_bytes=56 * 1024 * 1024),
    )(draws, factor)


def shards(factor, panels, base_demand, spread, head_base, head_drop, conductance, pipe_ends):
    local_rows, width = factor.shape
    n_row = lax.axis_size("row")
    n_col = lax.axis_size("col")
    if n_row == 4:
        partial_scores = gathered_scores(panels.T, factor)
        summed = lax.psum_scatter(partial_scores, "col", scatter_dimension=0, tiled=True)
        shares = summed.reshape(n_row, -1, local_rows)
        scores = lax.all_to_all(shares, "row", split_axis=0, concat_axis=0, tiled=True)
        return residual(scores, base_demand, spread, head_base, head_drop, conductance, pipe_ends)
    slab = local_rows * n_row
    offset = NODES - slab
    rows = lax.broadcasted_iota(jnp.int32, factor.shape, 0) + offset + lax.axis_index("row") * local_rows
    cols = lax.broadcasted_iota(jnp.int32, factor.shape, 1) + lax.axis_index("col") * width
    kept = jnp.where(cols <= rows, factor, jnp.zeros_like(factor))
    drawn = panels.shape[1]
    count = drawn // n_col
    part = count // HALVES
    draws = panels.T.reshape(drawn // count, HALVES, part, width)
    sums = []
    for h in range(HALVES):
        mine = draws[:, h].reshape(drawn // HALVES, width)
        every = lax.all_gather(mine, "row", axis=0, tiled=True)
        partial_scores = lax.dot_general(every, kept, (((1,), (1,)), ((), ())), preferred_element_type=jnp.float32)
        sums.append(lax.psum_scatter(partial_scores, "col", scatter_dimension=0, tiled=True))
    stacked = jnp.stack([s.reshape(n_row, part, local_rows) for s in sums], axis=1)
    stacked = stacked.reshape(n_row, count, local_rows)
    scores = lax.all_to_all(stacked, "row", split_axis=0, concat_axis=0, tiled=True)
    return residual(scores, base_demand, spread, head_base, head_drop, conductance, pipe_ends)


def solution(mesh):
    return jax.shard_map(
        shards,
        mesh=mesh,
        in_specs=(P("row", "col"), P("col", "row"), P(), P(), P(), P(), P(), P()),
        out_specs=P(("col", "row"), None),
        check_vma=False,
    )
```

time: 354 us -> 145 us (0.41)
  waiting for transfers between devices: 157 us -> 32.7 us
  other arithmetic: 91.1 us -> 0 us
  Pallas kernels: 0 us -> 89.5 us
  local copies, waits for them, and re-layouts: 69.9 us -> 0.02 us
  matrix products: 19 us -> 0 us
  blocking collectives: 0 us -> 8.76 us
  starting transfers between devices: 3.66 us -> 0.04 us
    all_gather x1 -> x0, waiting for transfers between devices: 92.1 us -> none  [shards(): lax.all_gather(panels, 'row', axis=1, tiled=True)]
    scatter-add x2 -> x0, other arithmetic: 89.9 us -> none  [shards(): jnp.zeros_like(demand).at[:, ends].add(flow).at[:, starts].add(-flow)]
    pallas_call x0 -> x2, Pallas kernels: none -> 89.5 us  [the longest x1 77 us: gathered_scores(): pl.pallas_call(gather_kernel, out_shape=jax.ShapeDtypeStruct((4 * drawn,...]
    gather x4 -> x0, local copies, waits for them, and re-layouts: 61.4 us -> none  [shards(): diff = jnp.take(heads, starts, axis=1) - jnp.take(heads, ends, axis=1)]
    psum x1 -> x0, waiting for transfers between devices: 58.8 us -> none  [shards(): summed = lax.psum(partial_scores, 'col')]
    reduce_scatter x0 -> x1, waiting for transfers between devices: none -> 32.7 us  [shards(): lax.psum_scatter(partial_scores, 'col', scatter_dimension=0, tiled=True)]
    dot_general x1 -> x0, matrix products: 19 us -> none  [shards(): lax.dot_general(lax.all_gather(panels, 'row', axis=1, tiled=True), kept,...]
    all_to_all x0 -> x1, blocking collectives: none -> 8.76 us  [shards(): lax.all_to_all(shares, 'row', split_axis=0, concat_axis=0, tiled=True)]
  transfers between devices with their start and end apart: 3 -> 1, of which waited for: 3 -> 1; matrix products, arithmetic and copies ran while one was open for 0% -> 0% of each run, Pallas kernels for 0% -> 0%
where the time goes in v1:
time: 145 us; the launch traced here: 144 us
  Pallas kernels  89.5 us (62%)
  waiting for transfers between devices  32.7 us (23%)
  between operations  13.4 us (9%)
  blocking collectives  8.76 us (6%)
    pallas_call x1, Pallas kernels, gathered_scores(): pl.pallas_call(gather_kernel, out_shape=jax.ShapeDtypeStruct((4 * drawn,...  77 us
    reduce_scatter x1, waiting for transfers between devices, shards(): lax.psum_scatter(partial_scores, 'col', scatter_dimension=0, tiled=True)  32.7 us
    pallas_call x1, Pallas kernels, residual(): pl.pallas_call(residual_kernel, grid=(pipes // PIPE_BLOCK,), out_shape=ja...  12.5 us
    all_to_all x1, blocking collectives, shards(): lax.all_to_all(shares, 'row', split_axis=0, concat_axis=0, tiled=True)  8.76 us
  transfers between devices with their start and end apart: 1, of which 1 were waited for; matrix products, arithmetic and copies ran while one was open for 0% of the time, Pallas kernels for 0%

profile of v1, /device:TPU:0, one launch (start us, length us, event | category | flops | bytes accessed | tf_op | source)
XLA Modules:
  0.0 144.4 jit_solution(4925109782137177681)
XLA Ops:
  6.5 0.0 copy-start
  6.5 0.0 copy-start.1
  6.5 0.0 copy-start.5
  6.5 0.0 copy-start.4
  6.5 0.0 copy-start.3
  6.5 0.0 copy-start.2
  6.6 0.0 reduce-scatter.2.cloned.1.call-start
  6.6 77.0 %shard_map.82 = f32[256,1024]{1,0:T(8,128)} custom-call(bf16[64,16384]{1,0:T(8,128)(2,1)} %bitcast.14, bf16[1024,16384]{1,0:T(8,128)(2,1)} %factor_ref.1), custom_call_target="tpu_custom_call" | custom-call | tf_op jit(solution)/shard_map/pallas_call | solution.py:250
  83.6 0.0 reduce-scatter.2.cloned.1.call-update
  83.6 32.7 %reduce-scatter.2.cloned.1.call-done = f32[32,1024]{1,0:T(8,128)} async-done(((f32[256,1024]{1,0:T(8,128)}), f32[32,1024]{1,0:T(8,128)}) %reduce-scatter.2.cloned.1.call-update) | async-done | bytes 131088 | tf_op jit(solution)/shard_map/reduce_scatter | solution.py:273
  116.3 8.8 %all_to_all.5.scores_ref = f32[4,8,1024]{2,1,0:T(8,128)S(1)} all-to-all(f32[4,8,1024]{2,1,0:T(8,128)} %bitcast.15), channel_id=1, replica_groups=mesh['row'=4,'col'=8] {'row'}, dimensions={0} | all-to-all | bytes 262144 | tf_op jit(solution)/shard_map/all_to_all | solution.py:275
  125.1 0.0 copy-done
  125.1 0.0 copy-done.1
  125.1 0.0 copy-done.5
  125.1 0.0 copy-done.4
  125.1 0.0 copy-done.3
  125.1 0.0 copy-done.2
  125.1 12.5 %shard_map.83 = f32[8,4096]{1,0:T(8,128)} custom-call(f32[4,8,1024]{2,1,0:T(8,128)S(1)} %all_to_all.5.scores_ref, f32[1,4096]{1,0:T(1,128)S(1)} %bitcast.10, f32[1,4096]{1,0:T(1,128)S(1)} %bitcast.11, f32[1,4096]{1,0:T(1,128)S(1)} %bitcast.12, f32[1,4096]{1,0:T(1,128)S(1)} %bitcast.13, f32[1,8192]{1,0:T(1,128)S(1)} %bitcast.9, s32[2,8192]{1,0:T(2,128)S(1)} %bitcast.8), custom_call_target="tpu_custom_call" | custom-call | tf_op jit(solution)/shard_map/pallas_call | solution.py:94
Async XLA Ops:
  6.5 118.5 %copy-start = (s32[8192,2]{0,1:T(2,128)S(1)}, s32[8192,2]{0,1:T(2,128)}, u32[]{:S(2)}) copy-start(s32[8192,2]{0,1:T(2,128)} %param.15) | copy-start | bytes 196612
  6.5 118.5 %copy-start.1 = (f32[8192]{0:T(1024)S(1)}, f32[8192]{0:T(1024)}, u32[]{:S(2)}) copy-start(f32[8192]{0:T(1024)} %param.14) | copy-start | bytes 98308
  6.5 118.5 %copy-start.5 = (f32[4096]{0:T(1024)S(1)}, f32[4096]{0:T(1024)}, u32[]{:S(2)}) copy-start(f32[4096]{0:T(1024)} %param.13) | copy-start | bytes 49156
  6.5 118.5 %copy-start.4 = (f32[4096]{0:T(1024)S(1)}, f32[4096]{0:T(1024)}, u32[]{:S(2)}) copy-start(f32[4096]{0:T(1024)} %param.12) | copy-start | bytes 49156
  6.5 118.6 %copy-start.3 = (f32[4096]{0:T(1024)S(1)}, f32[4096]{0:T(1024)}, u32[]{:S(2)}) copy-start(f32[4096]{0:T(1024)} %param.11) | copy-start | bytes 49156
  6.5 118.6 %copy-start.2 = (f32[4096]{0:T(1024)S(1)}, f32[4096]{0:T(1024)}, u32[]{:S(2)}) copy-start(f32[4096]{0:T(1024)} %param.10) | copy-start | bytes 49156
  6.6 109.8 %reduce-scatter.2.cloned.1.call-start = ((), (), s32[]{:S(2)}) async-start(), calls=%async_computation.2 | async-start | bytes 1179648 | tf_op jit(solution)/shard_map/reduce_scatter | solution.py:273
Sparse Core Ops, SparseCore 0:
  83.7 32.5 reduce-scatter.1

commit v2 on v1

--- a/solution.py
+++ b/solution.py
@@ -264,15 +264,116 @@
     )(draws, factor)
 
 
+def reduce_kernel(part_ref, out_ref, paired, landed, total, got, pair_send, pair_recv, z_send, z_recv, row_send, row_recv):
+    chips, share, _ = paired.shape
+    n_row, count, _ = got.shape
+    me = lax.axis_index("row")
+    column = lax.axis_index("col")
+    z = column // 2
+    core = column % 2
+    sibling = column + 1 - 2 * core
+
+    barrier = pltpu.get_barrier_semaphore()
+    peers = [{"col": sibling}]
+    peers += [{"col": ((z + d) % chips) * 2 + core} for d in range(1, chips)]
+    peers += [{"row": (me + d) % n_row} for d in range(1, n_row)]
+    for peer in peers:
+        pl.semaphore_signal(barrier, inc=1, device_id=peer, device_id_type=MESH)
+    pl.semaphore_wait(barrier, len(peers))
+
+    def block(d, side):
+        start = (((z + d) % chips) * 2 + side) * share
+        return pl.ds(pl.multiple_of(start, share), share)
+
+    order = list(range(1, chips)) + [0]
+    pairs = {}
+    for d in order:
+        pairs[d] = pltpu.make_async_remote_copy(
+            src_ref=part_ref.at[block(d, 1 - core), :],
+            dst_ref=paired.at[d],
+            send_sem=pair_send.at[d],
+            recv_sem=pair_recv.at[d],
+            device_id={"col": sibling},
+            device_id_type=MESH,
+        )
+        pairs[d].start()
+    hops = []
+    for d in order:
+        pairs[d].wait_recv()
+        if d == 0:
+            total[...] = paired[0] + part_ref[block(0, core), :]
+            continue
+        paired[d] = paired[d] + part_ref[block(d, core), :]
+        hop = pltpu.make_async_remote_copy(
+            src_ref=paired.at[d],
+            dst_ref=landed.at[d - 1],
+            send_sem=z_send.at[d - 1],
+            recv_sem=z_recv.at[d - 1],
+            device_id={"col": ((z + d) % chips) * 2 + core},
+            device_id_type=MESH,
+        )
+        hop.start()
+        hops.append(hop)
+    for d, hop in enumerate(hops):
+        hop.wait_recv()
+        total[...] = total[...] + landed[d]
+    moves = []
+    for d in range(1, n_row):
+        target = (me + d) % n_row
+        move = pltpu.make_async_remote_copy(
+            src_ref=total.at[pl.ds(pl.multiple_of(target * count, count), count), :],
+            dst_ref=got.at[me],
+            send_sem=row_send.at[d - 1],
+            recv_sem=row_recv.at[d - 1],
+            device_id={"row": target},
+            device_id_type=MESH,
+        )
+        move.start()
+        moves.append(move)
+    out_ref[me] = total[pl.ds(pl.multiple_of(me * count, count), count), :]
+    for d, move in enumerate(moves):
+        move.wait_recv()
+        source = (me + n_row - d - 1) % n_row
+        out_ref[source] = got[source]
+    for d in order:
+        pairs[d].wait_send()
+    for copy in hops + moves:
+        copy.wait_send()
+
+
+def reduced_scores(partial_scores, n_row, n_col):
+    scenarios, local_rows = partial_scores.shape
+    chips = n_col // 2
+    share = scenarios // n_col
+    count = share // n_row
+    return pl.pallas_call(
+        reduce_kernel,
+        out_shape=jax.ShapeDtypeStruct((n_row, count, local_rows), jnp.float32),
+        in_specs=[pl.BlockSpec(memory_space=pltpu.VMEM)],
+        out_specs=pl.BlockSpec(memory_space=pltpu.VMEM),
+        scratch_shapes=[
+            pltpu.VMEM((chips, share, local_rows), jnp.float32),
+            pltpu.VMEM((chips - 1, share, local_rows), jnp.float32),
+            pltpu.VMEM((share, local_rows), jnp.float32),
+            pltpu.VMEM((n_row, count, local_rows), jnp.float32),
+            pltpu.SemaphoreType.DMA((chips,)),
+            pltpu.SemaphoreType.DMA((chips,)),
+            pltpu.SemaphoreType.DMA((chips - 1,)),
+            pltpu.SemaphoreType.DMA((chips - 1,)),
+            pltpu.SemaphoreType.DMA((n_row - 1,)),
+            pltpu.SemaphoreType.DMA((n_row - 1,)),
+        ],
+        compiler_params=pltpu.CompilerParams(collective_id=1, has_side_effects=True, vmem_limit_bytes=32 * 1024 * 1024),
+    )(partial_scores)
+
+
 def shards(factor, panels, base_demand, spread, head_base, head_drop, conductance, pipe_ends):
     local_rows, width = factor.shape
     n_row = lax.axis_size("row")
     n_col = lax.axis_size("col")
     if n_row == 4:
         partial_scores = gathered_scores(panels.T, factor)
-        summed = lax.psum_scatter(partial_scores, "col", scatter_dimension=0, tiled=True)
-        shares = summed.reshape(n_row, -1, local_rows)
-        scores = lax.all_to_all(shares, "row", split_axis=0, concat_axis=0, tiled=True)
+        scores = reduced_scores(partial_scores, n_row, n_col)
         return residual(scores, base_demand, spread, head_base, head_drop, conductance, pipe_ends)
     slab = local_rows * n_row
     offset = NODES - slab

time: 145 us -> 109 us (0.75)
  waiting for transfers between devices: 32.7 us -> 0 us
  Pallas kernels: 89.5 us -> 107 us
  between operations: 13.4 us -> 0.09 us
  blocking collectives: 8.76 us -> 0 us
    reduce_scatter x1 -> x0, waiting for transfers between devices: 32.7 us -> none  [shards(): lax.psum_scatter(partial_scores, 'col', scatter_dimension=0, tiled=True)]
    pallas_call x0 -> x1, Pallas kernels: none -> 17.1 us  [reduced_scores(): pl.pallas_call(reduce_kernel, out_shape=jax.ShapeDtypeStruct((n_row, coun...]
    all_to_all x1 -> x0, blocking collectives: 8.76 us -> none  [shards(): lax.all_to_all(shares, 'row', split_axis=0, concat_axis=0, tiled=True)]
  transfers between devices with their start and end apart: 1 -> 0, of which waited for: 1 -> 0; matrix products, arithmetic and copies ran while one was open for 0% -> 0% of each run, Pallas kernels for 0% -> 0%
where the time goes in v2:
time: 109 us; the launch traced here: 108 us
  Pallas kernels  107 us (98%)
  local copies, waits for them, and re-layouts  1.24 us (1%)
    pallas_call x1, Pallas kernels, gathered_scores(): pl.pallas_call(gather_kernel, out_shape=jax.ShapeDtypeStruct((4 * drawn,...  77 us
    pallas_call x1, Pallas kernels, reduced_scores(): pl.pallas_call(reduce_kernel, out_shape=jax.ShapeDtypeStruct((n_row, coun...  17.1 us
    pallas_call x1, Pallas kernels, residual(): pl.pallas_call(residual_kernel, grid=(pipes // PIPE_BLOCK,), out_shape=ja...  12.5 us

profile of v2, /device:TPU:0, one launch (start us, length us, event | category | flops | bytes accessed | tf_op | source)
XLA Modules:
  0.0 107.9 jit_solution(9657363851670709862)
XLA Ops:
  0.0 0.0 copy-start.1
  0.0 0.0 copy-start.2
  0.0 0.0 copy-start.6
  0.0 0.0 copy-start.5
  0.0 0.0 copy-start.4
  0.0 0.0 copy-start.3
  0.0 77.0 %shard_map.82.part_ref = f32[256,1024]{1,0:T(8,128)} custom-call(bf16[64,16384]{1,0:T(8,128)(2,1)} %bitcast.13, bf16[1024,16384]{1,0:T(8,128)(2,1)} %factor_ref.1), custom_call_target="tpu_custom_call" | custom-call | tf_op jit(solution)/shard_map/pallas_call | solution.py:250
  77.0 0.0 copy-start
  77.0 1.2 %copy-done = f32[256,1024]{1,0:T(8,128)S(1)} copy-done((f32[256,1024]{1,0:T(8,128)S(1)}, f32[256,1024]{1,0:T(8,128)}, u32[]{:S(2)}) %copy-start) | copy-done | bytes 1048600
  78.3 17.1 %shard_map.83.scores_ref = f32[4,8,1024]{2,1,0:T(8,128)S(1)} custom-call(f32[256,1024]{1,0:T(8,128)S(1)} %copy-done), custom_call_target="tpu_custom_call" | custom-call | tf_op jit(solution)/shard_map/pallas_call | solution.py:349
  95.4 0.0 copy-done.1
  95.4 0.0 copy-done.2
  95.4 0.0 copy-done.6
  95.4 0.0 copy-done.5
  95.4 0.0 copy-done.4
  95.4 0.0 copy-done.3
  95.4 12.5 %shard_map.84 = f32[8,4096]{1,0:T(8,128)} custom-call(f32[4,8,1024]{2,1,0:T(8,128)S(1)} %shard_map.83.scores_ref, f32[1,4096]{1,0:T(1,128)S(1)} %bitcast.9, f32[1,4096]{1,0:T(1,128)S(1)} %bitcast.10, f32[1,4096]{1,0:T(1,128)S(1)} %bitcast.11, f32[1,4096]{1,0:T(1,128)S(1)} %bitcast.12, f32[1,8192]{1,0:T(1,128)S(1)} %bitcast.8, s32[2,8192]{1,0:T(2,128)S(1)} %bitcast.7), custom_call_target="tpu_custom_call" | custom-call | tf_op jit(solution)/shard_map/pallas_call | solution.py:94
Async XLA Ops:
  0.0 95.4 %copy-start.1 = (s32[8192,2]{0,1:T(2,128)S(1)}, s32[8192,2]{0,1:T(2,128)}, u32[]{:S(2)}) copy-start(s32[8192,2]{0,1:T(2,128)} %param.15) | copy-start | bytes 196612
  0.0 95.4 %copy-start.2 = (f32[8192]{0:T(1024)S(1)}, f32[8192]{0:T(1024)}, u32[]{:S(2)}) copy-start(f32[8192]{0:T(1024)} %param.14) | copy-start | bytes 98308
  0.0 95.4 %copy-start.6 = (f32[4096]{0:T(1024)S(1)}, f32[4096]{0:T(1024)}, u32[]{:S(2)}) copy-start(f32[4096]{0:T(1024)} %param.13) | copy-start | bytes 49156
  0.0 95.4 %copy-start.5 = (f32[4096]{0:T(1024)S(1)}, f32[4096]{0:T(1024)}, u32[]{:S(2)}) copy-start(f32[4096]{0:T(1024)} %param.12) | copy-start | bytes 49156
  0.0 95.4 %copy-start.4 = (f32[4096]{0:T(1024)S(1)}, f32[4096]{0:T(1024)}, u32[]{:S(2)}) copy-start(f32[4096]{0:T(1024)} %param.11) | copy-start | bytes 49156
  0.0 95.4 %copy-start.3 = (f32[4096]{0:T(1024)S(1)}, f32[4096]{0:T(1024)}, u32[]{:S(2)}) copy-start(f32[4096]{0:T(1024)} %param.10) | copy-start | bytes 49156
  77.0 1.2 %copy-start = (f32[256,1024]{1,0:T(8,128)S(1)}, f32[256,1024]{1,0:T(8,128)}, u32[]{:S(2)}) copy-start(f32[256,1024]{1,0:T(8,128)} %shard_map.82.part_ref) | copy-start | bytes 3145732
